TPU v7x, 32 devices: a whole 2x2x4 slice. The times are simulated.
32 devices in a mesh: mem: 2 (over x), lat: 4 (over z), lon: 4 (over y, core).
Axes of the slice: x: 2, y: 2, z: 4, core: 2. Of those that a mesh axis runs over, the one named last changes fastest.
Arguments:
- control: bfloat16 [8, 256, 128, 128], P('mem', 'lat', 'lon'), may hold values from -21 to 21
- ensemble: bfloat16 [8, 256, 128, 128], P('mem', 'lat', 'lon'), may hold values from -3 to 3
- precision: float32 [256, 128, 128], P('lat', 'lon'), may hold values from 0.5 to 8
- lat_taps: float32 [9], replicated, may hold values from 0.05 to 0.3
- lon_taps: float32 [9], replicated, may hold values from 0.05 to 0.3
- vertical: bfloat16 [128, 128], replicated, may hold values from -0.5 to 0.5
Outputs:
- hessian: float32 [8, 256, 128, 128], P('mem', 'lat', 'lon')
- curvature: float32 [], replicated
All inputs are finite; a program needn't handle non-finite values.
Results may differ from a plain program's by a relative error of at most 0.0038.
Values may be sent and summed in bfloat16 or wider, within the bound.
A program may use at most 64 MiB of HBM per device.

v0:
```python
import jax
import jax.numpy as jnp
from jax import lax
from jax.sharding import PartitionSpec as P


def extended_2(value, sides, width):
    for axis, dim in sides:
        peers, length = (lax.axis_size(axis), value.shape[dim])
        up = [(i, (i + 1) % peers) for i in range(peers)]
        down = [(j, i) for i, j in up]
        last = lax.slice_in_dim(value, length - width, length, axis=dim)
        initial = lax.slice_in_dim(value, 0, width, axis=dim)
        before = lax.ppermute(last, axis, up)
        after = lax.ppermute(initial, axis, down)
        value = jnp.concatenate([before, value, after], axis=dim)
    return value


def smooth_block(extended, first_taps, second_taps, tile_rows, tile_cols):
    across = first_taps[0] * extended[:, 0:tile_rows]
    for offset in range(1, first_taps.shape[0]):
        across = across + first_taps[offset] * extended[:, offset : offset + tile_rows]
    result = second_taps[0] * across[:, :, 0:tile_cols]
    for offset in range(1, second_taps.shape[0]):
        result = result + second_taps[offset] * across[:, :, offset : offset + tile_cols]
    return result


def clear_edges(extended, tile_rows):
    lat_pos = lax.axis_index("lat")
    lat_count = lax.axis_size("lat")
    row_index = jnp.arange(tile_rows + 8)
    outside = jnp.logical_or(
        jnp.logical_and(row_index < 4, lat_pos == 0),
        jnp.logical_and(row_index >= tile_rows + 4, lat_pos == lat_count - 1),
    )
    return jnp.where(outside[None, :, None, None], jnp.zeros((), extended.dtype), extended)


def per_device(control, ensemble, precision, lat_taps, lon_taps, vertical):
    tile_rows = control.shape[1]
    tile_cols = control.shape[2]
    levels = control.shape[3]
    entries = control.size * lax.axis_size("mem") * lax.axis_size("lat") * lax.axis_size("lon")
    extended = extended_2(control, (("lat", 1), ("lon", 2)), 4)
    extended = clear_edges(extended, tile_rows)
    smoothed = smooth_block(extended, lat_taps, lon_taps, tile_rows, tile_cols).astype(jnp.bfloat16)
    leveled = jnp.dot(
        smoothed.reshape(-1, levels), vertical, preferred_element_type=jnp.float32
    ).reshape(smoothed.shape)
    partial_value = jnp.sum(ensemble * leveled, axis=0)
    increment = lax.psum(partial_value, "mem")
    weighted = precision * increment
    member_part = (ensemble * weighted[None]).astype(jnp.bfloat16)
    adjoint_lev = lax.dot_general(
        member_part.reshape(-1, levels),
        vertical,
        (((1,), (1,)), ((), ())),
        preferred_element_type=jnp.float32,
    )
    adjoint_lev = adjoint_lev.reshape(member_part.shape).astype(jnp.bfloat16)
    adjoint_ext = extended_2(adjoint_lev, (("lat", 1), ("lon", 2)), 4)
    adjoint_ext = clear_edges(adjoint_ext, tile_rows)
    back = smooth_block(adjoint_ext, lat_taps[::-1], lon_taps[::-1], tile_rows, tile_cols)
    hessian = control + back
    curvature = lax.psum(jnp.sum(control * hessian), ("mem", "lat", "lon")) / entries
    return (hessian, curvature)


def solution(mesh):
    in_specs = (
        P("mem", "lat", "lon", None),
        P("mem", "lat", "lon", None),
        P("lat", "lon", None),
        P(),
        P(),
        P(),
    )
    out_specs = (P("mem", "lat", "lon", None), P())
    return jax.shard_map(
        per_device, mesh=mesh, in_specs=in_specs, out_specs=out_specs, check_vma=False
    )
```

profile of v0, /device:TPU:0, one launch (start us, length us, event | category | flops | bytes accessed | tf_op | source)
XLA Modules:
  0.0 218.0 jit_solution(198119640053261836)
XLA Ops:
  7.2 1.0 fusion.31
  8.2 3.1 %collective-permute-start = (bf16[4,4,32,128]{3,2,1,0:T(8,128)(2,1)S(1)}, bf16[4,4,32,128]{3,2,1,0:T(8,128)(2,1)S(1)}, u32[]{:S(2)}, u32[]{:S(2)}) collective-permute-start(bf16[4,4,32,128]{3,2,1,0:T(8,128)(2,1)S(1)} %get-tuple-element.11), channel_id=1, source_target_pairs={{0,4},{4,8},{8,12},{12,0},{1,5},{5,9},{9,13},{13,1},{2,6},{6,10},{... | collective-permute-start | bytes 393224 | tf_op jit(solution)/shard_map/ppermute | solution.py:14
  11.3 2.1 collective-permute-start.1
  13.4 4.3 %collective-permute-done = bf16[4,4,32,128]{3,2,1,0:T(8,128)(2,1)S(1)} collective-permute-done((bf16[4,4,32,128]{3,2,1,0:T(8,128)(2,1)S(1)}, bf16[4,4,32,128]{3,2,1,0:T(8,128)(2,1)S(1)}, u32[]{:S(2)}, u32[]{:S(2)}) %collective-permute-start) | collective-permute-done | bytes 131104 | tf_op jit(solution)/shard_map/ppermute | solution.py:14
  17.7 2.2 constant_dynamic-update-slice_fusion.1
  20.3 1.7 collective-permute-start.3
  23.4 4.1 %collective-permute-done.2 = bf16[4,72,4,128]{3,2,1,0:T(4,128)(2,1)S(1)} collective-permute-done((bf16[4,72,4,128]{3,2,1,0:T(4,128)(2,1)S(1)}, bf16[4,72,4,128]{3,2,1,0:T(4,128)(2,1)S(1)}, u32[]{:S(2)}, u32[]{:S(2)}) %collective-permute-start.2) | collective-permute-done | bytes 294944 | tf_op jit(solution)/shard_map/ppermute | solution.py:14
  27.5 1.3 collective-permute-done.3
  28.8 2.2 %maximum_select_fusion = bf16[4,72,40,128]{3,2,1,0:T(8,128)(2,1)S(1)} fusion(bf16[4,72,4,128]{3,2,1,0:T(4,128)(2,1)S(1)} %collective-permute-done.3, bf16[4,72,32,128]{3,2,1,0:T(8,128)(2,1)S(1)} %constant_dynamic-update-slice_fusion, bf16[4,72,4,128]{3,2,1,0:T(4,128)(2,1)S(1)} %collective-permute-done.2, pred[72]{0:T(512)(128)(4,1)S(1)} %and_or_fusion), kind=kLoop, calls=%fused_computation.44 | loop fusion | flops 10321920 | bytes 5898312 | tf_op jit(solution)/shard_map/jit(_where)/select_n | solution.py:38
  31.1 11.4 %multiply_add_fusion.1 = f32[4,64,40,128]{3,2,1,0:T(8,128)} fusion(bf16[4,72,40,128]{3,2,1,0:T(8,128)(2,1)S(1)} %maximum_select_fusion, f32[]{:T(128)} %bitcast.10, f32[]{:T(128)} %bitcast.9, f32[]{:T(128)} %bitcast.8, f32[]{:T(128)} %bitcast.7, f32[]{:T(128)} %bitcast.6, f32[]{:T(128)} %bitcast.5, f32[]{:T(128)} %bitcast.4, f32[]{:T(128)} %bitcast.3, f32[]{:T(128)} %bitcast.1), kind=kLoop, calls=%fused_computation.5 | loop fusion | flops 34078720 | bytes 28835876 | tf_op jit(solution)/shard_map/add | solution.py:23
  42.4 24.0 %fusion.1 = f32[64,32,128]{2,1,0:T(8,128)} fusion(bf16[4,64,32,128]{3,2,1,0:T(8,128)(2,1)S(1)} %copy-done.2, f32[4,64,40,128]{3,2,1,0:T(8,128)} %multiply_add_fusion.1, f32[]{:T(128)} %bitcast.17, f32[]{:T(128)} %bitcast.16, f32[]{:T(128)} %bitcast.15, f32[]{:T(128)} %bitcast.14, f32[]{:T(128)} %bitcast.13, f32[]{:T(128)} %bitcast.12, f32[]{:T(128)} %bitcast.11, ...), kind=kOutput, calls=%fused_computation.7 | convolution fusion | flops 290193408 | bytes 40931840 | tf_op jit(solution)/shard_map/dot_general | solution.py:49
  66.5 41.8 %all-reduce.2.cloned.1.call-done = f32[64,32,128]{2,1,0:T(8,128)} async-done(((f32[64,32,128]{2,1,0:T(8,128)}), f32[64,32,128]{2,1,0:T(8,128)}) %all-reduce.2.cloned.1.call-update) | async-done | bytes 1048592 | tf_op jit(solution)/shard_map/psum | solution.py:53
  108.3 1.4 mul.234
  110.5 1.5 collective-permute-start.4
  112.0 2.3 %collective-permute-start.5 = (bf16[4,4,32,128]{3,2,1,0:T(8,128)(2,1)S(1)}, bf16[4,4,32,128]{3,2,1,0:T(8,128)(2,1)S(1)}, u32[]{:S(2)}, u32[]{:S(2)}) collective-permute-start(bf16[4,4,32,128]{3,2,1,0:T(8,128)(2,1)S(1)} %get-tuple-element.9), channel_id=1, source_target_pairs={{4,0},{8,4},{12,8},{0,12},{5,1},{9,5},{13,9},{1,13},{6,2},{10,6},{... | collective-permute-start | bytes 393224 | tf_op jit(solution)/shard_map/ppermute | solution.py:15
  114.4 4.3 %collective-permute-done.4 = bf16[4,4,32,128]{3,2,1,0:T(8,128)(2,1)S(1)} collective-permute-done((bf16[4,4,32,128]{3,2,1,0:T(8,128)(2,1)S(1)}, bf16[4,4,32,128]{3,2,1,0:T(8,128)(2,1)S(1)}, u32[]{:S(2)}, u32[]{:S(2)}) %collective-permute-start.4) | collective-permute-done | bytes 131104 | tf_op jit(solution)/shard_map/ppermute | solution.py:14
  118.7 0.9 collective-permute-done.5
  119.9 1.7 collective-permute-start.7
  121.7 5.8 %collective-permute-done.6 = bf16[4,72,4,128]{3,2,1,0:T(4,128)(2,1)S(1)} collective-permute-done((bf16[4,72,4,128]{3,2,1,0:T(4,128)(2,1)S(1)}, bf16[4,72,4,128]{3,2,1,0:T(4,128)(2,1)S(1)}, u32[]{:S(2)}, u32[]{:S(2)}) %collective-permute-start.6) | collective-permute-done | bytes 294944 | tf_op jit(solution)/shard_map/ppermute | solution.py:14
  127.5 0.8 collective-permute-done.7
  128.2 3.5 %maximum_select_fusion.1 = bf16[4,72,40,128]{3,2,1,0:T(8,128)(2,1)S(1)} fusion(bf16[4,72,4,128]{3,2,1,0:T(4,128)(2,1)S(1)} %collective-permute-done.7, bf16[4,4,32,128]{3,2,1,0:T(8,128)(2,1)S(1)} %collective-permute-done.5, bf16[4,64,32,128]{3,2,1,0:T(8,128)(2,1)S(1)} %fusion.24, bf16[4,4,32,128]{3,2,1,0:T(8,128)(2,1)S(1)} %collective-permute-done.4, ...), kind=kLoop, calls=%fused_computation.45 | loop fusion | flops 16220160 | bytes 5898312 | tf_op jit(solution)/shard_map/jit(_where)/select_n | solution.py:38
  131.7 11.4 %multiply_add_fusion = f32[4,64,40,128]{3,2,1,0:T(8,128)} fusion(bf16[4,72,40,128]{3,2,1,0:T(8,128)(2,1)S(1)} %maximum_select_fusion.1, f32[]{:T(128)} %bitcast.10, f32[]{:T(128)} %bitcast.9, f32[]{:T(128)} %bitcast.8, f32[]{:T(128)} %bitcast.7, f32[]{:T(128)} %bitcast.6, f32[]{:T(128)} %bitcast.5, f32[]{:T(128)} %bitcast.4, f32[]{:T(128)} %bitcast.3, f32[]{:T(128)} %bitcast.1), kind=kLoop, calls=%fused_computation.4 | loop fusion | flops 34078720 | bytes 28835876 | tf_op jit(solution)/shard_map/add | solution.py:23
  143.1 27.1 %fusion = (f32[]{:T(128)}, f32[4,64,32,128]{3,2,1,0:T(8,128)}) fusion(bf16[4,64,32,128]{3,2,1,0:T(8,128)(2,1)S(1)} %copy-done.1, f32[4,64,40,128]{3,2,1,0:T(8,128)} %multiply_add_fusion, f32[]{:T(128)} %bitcast.2, f32[]{:T(128)} %bitcast.11, f32[]{:T(128)} %bitcast.12, f32[]{:T(128)} %bitcast.13, f32[]{:T(128)} %bitcast.14, f32[]{:T(128)} %bitcast.15, ...), kind=kLoop, calls=%fused_computation.6 | loop fusion | flops 22020096 | bytes 44040232 | tf_op jit(solution)/shard_map/reduce_sum | solution.py:67
  170.1 39.3 %psum.15 = f32[]{:T(128)} all-reduce(f32[]{:T(128)} %get-tuple-element.2), channel_id=1, replica_groups=mesh['mem'=2,'lat'=4,'lon'=4] {'mem','lat','lon'}, use_global_device_ids=true, to_apply=%region_3.4 | all-reduce | flops 1 | bytes 8 | tf_op jit(solution)/shard_map/psum | solution.py:67
  (26 shorter events, 2.8 us)
Async XLA Ops:
  7.2 35.3 %copy-start = (bf16[128,128]{1,0:T(8,128)(2,1)S(1)}, bf16[128,128]{1,0:T(8,128)(2,1)}, u32[]{:S(2)}) copy-start(bf16[128,128]{1,0:T(8,128)(2,1)} %param.11) | copy-start | bytes 98308
  7.2 14.8 %copy-start.4 = (f32[9]{0:T(128)S(1)}, f32[9]{0:T(128)}, u32[]{:S(2)}) copy-start(f32[9]{0:T(128)} %param.9) | copy-start | bytes 112
  7.2 15.5 %copy-start.5 = (f32[9]{0:T(128)S(1)}, f32[9]{0:T(128)}, u32[]{:S(2)}) copy-start(f32[9]{0:T(128)} %param.10) | copy-start | bytes 112
  7.2 101.1 %all-reduce.2.cloned.1.call-start = ((), (), s32[]{:S(2)}) async-start(), calls=%async_computation | async-start | bytes 2097152 | tf_op jit(solution)/shard_map/psum | solution.py:53
  8.2 9.5 %collective-permute-start = (bf16[4,4,32,128]{3,2,1,0:T(8,128)(2,1)S(1)}, bf16[4,4,32,128]{3,2,1,0:T(8,128)(2,1)S(1)}, u32[]{:S(2)}, u32[]{:S(2)}) collective-permute-start(bf16[4,4,32,128]{3,2,1,0:T(8,128)(2,1)S(1)} %get-tuple-element.11), channel_id=1, source_target_pairs={{0,4},{4,8},{8,12},{12,0},{1,5},{5,9},{9,13},{13,1},{2,6},{6,10},{... | collective-permute-start | bytes 393224 | tf_op jit(solution)/shard_map/ppermute | solution.py:14
  11.3 8.6 %collective-permute-start.1 = (bf16[4,4,32,128]{3,2,1,0:T(8,128)(2,1)S(1)}, bf16[4,4,32,128]{3,2,1,0:T(8,128)(2,1)S(1)}, u32[]{:S(2)}, u32[]{:S(2)}) collective-permute-start(bf16[4,4,32,128]{3,2,1,0:T(8,128)(2,1)S(1)} %get-tuple-element.10), channel_id=1, source_target_pairs={{4,0},{8,4},{12,8},{0,12},{5,1},{9,5},{13,9},{1,13},{6,2},{10,6},{... | collective-permute-start | bytes 393224 | tf_op jit(solution)/shard_map/ppermute | solution.py:15
  20.2 7.3 %collective-permute-start.2 = (bf16[4,72,4,128]{3,2,1,0:T(4,128)(2,1)S(1)}, bf16[4,72,4,128]{3,2,1,0:T(4,128)(2,1)S(1)}, u32[]{:S(2)}, u32[]{:S(2)}) collective-permute-start(bf16[4,72,4,128]{3,2,1,0:T(4,128)(2,1)S(1)} %get-tuple-element.6), channel_id=1, source_target_pairs={{0,1},{1,2},{2,3},{3,0},{4,5},{5,6},{6,7},{7,4},{8,9},{9,10},{10,1... | collective-permute-start | bytes 884744 | tf_op jit(solution)/shard_map/ppermute | solution.py:14
  20.3 8.5 %collective-permute-start.3 = (bf16[4,72,4,128]{3,2,1,0:T(4,128)(2,1)S(1)}, bf16[4,72,4,128]{3,2,1,0:T(4,128)(2,1)S(1)}, u32[]{:S(2)}, u32[]{:S(2)}) collective-permute-start(bf16[4,72,4,128]{3,2,1,0:T(4,128)(2,1)S(1)} %get-tuple-element.7), channel_id=1, source_target_pairs={{1,0},{2,1},{3,2},{0,3},{5,4},{6,5},{7,6},{4,7},{9,8},{10,9},{11,1... | collective-permute-start | bytes 884744 | tf_op jit(solution)/shard_map/ppermute | solution.py:15
  31.1 11.4 %copy-start.2 = (bf16[4,64,32,128]{3,2,1,0:T(8,128)(2,1)S(1)}, bf16[4,64,32,128]{3,2,1,0:T(8,128)(2,1)}, u32[]{:S(2)}) copy-start(bf16[4,64,32,128]{3,2,1,0:T(8,128)(2,1)} %param.7) | copy-start | bytes 6291460
  42.4 65.8 %copy-start.3 = (f32[64,32,128]{2,1,0:T(8,128)S(1)}, f32[64,32,128]{2,1,0:T(8,128)}, u32[]{:S(2)}) copy-start(f32[64,32,128]{2,1,0:T(8,128)} %param.8) | copy-start | bytes 3145732
  110.5 8.2 %collective-permute-start.4 = (bf16[4,4,32,128]{3,2,1,0:T(8,128)(2,1)S(1)}, bf16[4,4,32,128]{3,2,1,0:T(8,128)(2,1)S(1)}, u32[]{:S(2)}, u32[]{:S(2)}) collective-permute-start(bf16[4,4,32,128]{3,2,1,0:T(8,128)(2,1)S(1)} %get-tuple-element.8), channel_id=1, source_target_pairs={{0,4},{4,8},{8,12},{12,0},{1,5},{5,9},{9,13},{13,1},{2,6},{6,10},{... | collective-permute-start | bytes 393224 | tf_op jit(solution)/shard_map/ppermute | solution.py:14
  112.0 7.6 %collective-permute-start.5 = (bf16[4,4,32,128]{3,2,1,0:T(8,128)(2,1)S(1)}, bf16[4,4,32,128]{3,2,1,0:T(8,128)(2,1)S(1)}, u32[]{:S(2)}, u32[]{:S(2)}) collective-permute-start(bf16[4,4,32,128]{3,2,1,0:T(8,128)(2,1)S(1)} %get-tuple-element.9), channel_id=1, source_target_pairs={{4,0},{8,4},{12,8},{0,12},{5,1},{9,5},{13,9},{1,13},{6,2},{10,6},{... | collective-permute-start | bytes 393224 | tf_op jit(solution)/shard_map/ppermute | solution.py:15
  119.9 7.6 %collective-permute-start.6 = (bf16[4,72,4,128]{3,2,1,0:T(4,128)(2,1)S(1)}, bf16[4,72,4,128]{3,2,1,0:T(4,128)(2,1)S(1)}, u32[]{:S(2)}, u32[]{:S(2)}) collective-permute-start(bf16[4,72,4,128]{3,2,1,0:T(4,128)(2,1)S(1)} %get-tuple-element.4), channel_id=1, source_target_pairs={{0,1},{1,2},{2,3},{3,0},{4,5},{5,6},{6,7},{7,4},{8,9},{9,10},{10,1... | collective-permute-start | bytes 884744 | tf_op jit(solution)/shard_map/ppermute | solution.py:14
  119.9 8.3 %collective-permute-start.7 = (bf16[4,72,4,128]{3,2,1,0:T(4,128)(2,1)S(1)}, bf16[4,72,4,128]{3,2,1,0:T(4,128)(2,1)S(1)}, u32[]{:S(2)}, u32[]{:S(2)}) collective-permute-start(bf16[4,72,4,128]{3,2,1,0:T(4,128)(2,1)S(1)} %get-tuple-element.5), channel_id=1, source_target_pairs={{1,0},{2,1},{3,2},{0,3},{5,4},{6,5},{7,6},{4,7},{9,8},{10,9},{11,1... | collective-permute-start | bytes 884744 | tf_op jit(solution)/shard_map/ppermute | solution.py:15
  131.7 11.4 %copy-start.1 = (bf16[4,64,32,128]{3,2,1,0:T(8,128)(2,1)S(1)}, bf16[4,64,32,128]{3,2,1,0:T(8,128)(2,1)}, u32[]{:S(2)}) copy-start(bf16[4,64,32,128]{3,2,1,0:T(8,128)(2,1)} %param.6) | copy-start | bytes 6291460
Sparse Core Ops, SparseCore 0:
  66.6 41.6 all-reduce.1
where the time goes:
time: 219 us; the launch traced here: 218 us
  waiting for transfers between devices  63.3 us (29%)
  other arithmetic  57.2 us (26%)
  blocking collectives  39.3 us (18%)
  matrix products  24.8 us (11%)
  between operations  16 us (7%)
  starting transfers between devices  12.7 us (6%)
  local copies, waits for them, and re-layouts  4.86 us (2%)
    psum x1, waiting for transfers between devices, per_device(): increment = lax.psum(partial_value, 'mem')  41.8 us
    psum x1, blocking collectives, per_device(): lax.psum(jnp.sum(control * hessian), ('mem', 'lat', 'lon')) / entries  39.3 us
    reduce_sum x1, other arithmetic, per_device(): jnp.sum(control * hessian)  27.1 us
    dot_general x1, matrix products, per_device(): jnp.dot(smoothed.reshape(-1, levels), vertical, preferred_element_type=jn...  24 us
    add x2, other arithmetic, smooth_block(): across + first_taps[offset] * extended[:, offset:offset + tile_rows]  22.7 us
    ppermute x4, waiting for transfers between devices, extended_2(): before = lax.ppermute(last, axis, up)  18.6 us
    ppermute x4, starting transfers between devices, extended_2(): after = lax.ppermute(initial, axis, down)  7.89 us
    select_n x2, other arithmetic, clear_edges(): jnp.where(outside[None, :, None, None], jnp.zeros((), extended.dtype), ex...  5.7 us
  transfers between devices with their start and end apart: 9, of which 8 were waited for; matrix products, arithmetic and copies ran while one was open for 2% of the time, Pallas kernels for 0%

commit v1 on v0

v1 whole, which is shorter than its diff:
```python
import functools

import jax
import jax.numpy as jnp
from jax import lax
from jax.experimental import pallas as pl
from jax.experimental.pallas import tpu as pltpu
from jax.sharding import PartitionSpec as P

F32 = jnp.float32
BF16 = jnp.bfloat16
HALF = 4


def iota(shape, dim):
    return lax.broadcasted_iota(jnp.int32, shape, dim)


def filter_matrix(lat_taps, lon_taps, cols, reverse):
    taps = lat_taps.shape[0]
    shape = (HALF * cols, 3 * HALF * cols + 6 * HALF * HALF)
    out, src = iota(shape, 0), iota(shape, 1)
    main = 3 * HALF * cols
    side = 3 * HALF * HALF
    inside = src < main
    left = src < main + side
    packed = jnp.where(left, src - main, src - main - side)
    row = jnp.where(inside, src // cols, packed // HALF)
    col = jnp.where(
        inside, src % cols, packed % HALF + jnp.where(left, -HALF, cols)
    )
    down = row - out // cols
    across = col - out % cols + HALF
    first = jnp.zeros(shape, F32)
    second = jnp.zeros(shape, F32)
    for tap in range(taps):
        at = taps - 1 - tap if reverse else tap
        first = jnp.where(down == tap, lat_taps[at], first)
        second = jnp.where(across == tap, lon_taps[at], second)
    full = first * second
    high = full.astype(BF16)
    low = (full - high.astype(F32)).astype(BF16)
    return jnp.concatenate([high, low], axis=0)


def pack_matrix(cols):
    size = HALF * HALF
    shape = (2 * size, HALF * cols)
    out, src = iota(shape, 0), iota(shape, 1)
    place = out % size
    col = place % HALF + jnp.where(out < size, 0, cols - HALF)
    wanted = (place // HALF) * cols + col
    return jnp.where(src == wanted, 1.0, 0.0).astype(BF16)


def dot(a, b):
    return jnp.dot(a, b, preferred_element_type=F32)


def kernel(
    axes, sizes, entries, chunks, lat_taps, lon_taps, control, ensemble, precision, vertical, hess, curv,
    ext, ext2, ens, prec, own, inc_out, inc_in, halo, halo2, stage, stage2,
    filt, filt2, picks, vert, vert2, vert2t, sums, cs0, cs1, cs2,
    local_sem, send_sem, recv_sem, inc_send, inc_recv, cs_send, cs_recv,
):
    members, rows, cols, levels = control.shape
    groups = rows // HALF
    cells = HALF * cols
    width = 2 if members % 2 == 0 else 1
    me = {a: lax.axis_index(a) for a in axes}
    n = dict(zip(axes, sizes))

    def device(**at):
        return tuple(at.get(a, me[a]) for a in axes)

    lat, lon = me["lat"], me["lon"]
    left = lax.rem(lon + n["lon"] - 1, n["lon"])
    right = lax.rem(lon + 1, n["lon"])
    has_up = lat > 0
    has_down = lat < n["lat"] - 1

    loads = [
        pltpu.make_async_copy(control, ext.at[:, pl.ds(HALF, rows)], local_sem.at[0]),
        pltpu.make_async_copy(vertical, vert, local_sem.at[1]),
        pltpu.make_async_copy(ensemble, ens, local_sem.at[2]),
        pltpu.make_async_copy(precision, prec, local_sem.at[3]),
    ]
    for load in loads:
        load.start()

    barrier = pltpu.get_barrier_semaphore()
    fixed = 0
    for axis in axes:
        for step in range(1, n[axis]):
            to = device(**{axis: lax.rem(me[axis] + step, n[axis])})
            pl.semaphore_signal(barrier, inc=1, device_id=to, device_id_type=pl.DeviceIdType.MESH)
            fixed += 1
    for has, row in ((has_up, lat - 1), (has_down, lat + 1)):
        @pl.when(has)
        def _():
            for col in (left, right):
                pl.semaphore_signal(
                    barrier, inc=1, device_id=device(lat=row, lon=col), device_id_type=pl.DeviceIdType.MESH
                )
    corners = jnp.where(has_up, 2, 0) + jnp.where(has_down, 2, 0)
    pl.semaphore_wait(barrier, fixed + corners)

    def remote(src, dst, send, recv, to):
        return pltpu.make_async_remote_copy(
            src_ref=src, dst_ref=dst, send_sem=send, recv_sem=recv,
            device_id=to, device_id_type=pl.DeviceIdType.MESH,
        )

    def row_copies(phase, up_src, down_src, dst):
        up = remote(
            up_src, dst.at[:, pl.ds(rows + HALF, HALF)],
            send_sem.at[phase, 0], recv_sem.at[phase, 0], device(lat=lat - 1),
        )
        down = remote(
            down_src, dst.at[:, pl.ds(0, HALF)],
            send_sem.at[phase, 1], recv_sem.at[phase, 1], device(lat=lat + 1),
        )
        return [up], [down]

    def side_copies(phase, src, dst):
        flat, up, down = [], [], []
        for side, to in ((0, left), (1, right)):
            there = dst.at[1 - side]
            mine = src.at[side]
            flat.append(remote(
                mine, there.at[:, pl.ds(1, groups)],
                send_sem.at[phase, 2 + side], recv_sem.at[phase, 2 + side], device(lon=to),
            ))
            up.append(remote(
                mine.at[:, 0], there.at[:, groups + 1],
                send_sem.at[phase, 4 + side], recv_sem.at[phase, 4 + side], device(lat=lat - 1, lon=to),
            ))
            down.append(remote(
                mine.at[:, groups - 1], there.at[:, 0],
                send_sem.at[phase, 6 + side], recv_sem.at[phase, 6 + side], device(lat=lat + 1, lon=to),
            ))
        return flat, up, down

    def start(flat, up, down):
        @pl.when(has_up)
        def _():
            for copy in up:
                copy.start()

        @pl.when(has_down)
        def _():
            for copy in down:
                copy.start()

        for copy in flat:
            copy.start()

    def received(flat, up, down):
        @pl.when(has_up)
        def _():
            for copy in down:
                copy.wait_recv()

        @pl.when(has_down)
        def _():
            for copy in up:
                copy.wait_recv()

        for copy in flat:
            copy.wait_recv()

    def sent(flat, up, down):
        @pl.when(has_up)
        def _():
            for copy in up:
                copy.wait_send()

        @pl.when(has_down)
        def _():
            for copy in down:
                copy.wait_send()

        for copy in flat:
            copy.wait_send()

    row_up, row_down = row_copies(
        0, control.at[:, pl.ds(0, HALF)], control.at[:, pl.ds(rows - HALF, HALF)], ext
    )
    start([], row_up, row_down)

    @pl.when(jnp.logical_not(has_up))
    def _():
        for one, two in ((ext, halo), (ext2, halo2)):
            one[:, 0:HALF] = jnp.zeros((members, HALF, cols, levels), BF16)
            for side in range(2):
                two[side, :, 0] = jnp.zeros((members, HALF * HALF, levels), BF16)

    @pl.when(jnp.logical_not(has_down))
    def _():
        for one, two in ((ext, halo), (ext2, halo2)):
            one[:, rows + HALF : rows + 2 * HALF] = jnp.zeros((members, HALF, cols, levels), BF16)
            for side in range(2):
                two[side, :, groups + 1] = jnp.zeros((members, HALF * HALF, levels), BF16)

    picks[...] = pack_matrix(cols)
    loads[0].wait()

    def pack(blocks, go, dst):
        packed = dot(picks[...], jnp.concatenate(blocks, axis=1)).astype(BF16)
        size = HALF * HALF
        for m in range(members):
            lanes = slice(m * levels, (m + 1) * levels)
            dst[0, m, go] = packed[:size, lanes]
            dst[1, m, go] = packed[size:, lanes]

    def pack_group(go, carry):
        at = pl.ds(HALF * (go + 1), HALF)
        pack([ext[m, at].reshape(cells, levels) for m in range(members)], go, stage)
        return carry

    lax.fori_loop(0, groups, pack_group, 0, unroll=2)
    side_flat, side_up, side_down = side_copies(0, stage, halo)
    start(side_flat, side_up, side_down)

    filt[...] = filter_matrix(lat_taps, lon_taps, cols, False)
    filt2[...] = filter_matrix(lat_taps, lon_taps, cols, True)
    loads[1].wait()
    v = vert[...].astype(F32)
    vt = v.T
    blank = jnp.zeros((levels, levels), F32)

    def diagonal(block):
        if width == 1:
            return block.astype(BF16)
        return jnp.concatenate(
            [jnp.concatenate([block, blank], axis=1), jnp.concatenate([blank, block], axis=1)], axis=0
        ).astype(BF16)

    vert2[...] = diagonal(v)
    vert2t[...] = diagonal(vt)
    sums[...] = jnp.zeros_like(sums)
    loads[2].wait()
    loads[3].wait()

    def tile_sum(x):
        return jnp.sum(x.reshape(-1, 8, levels), axis=0)

    def smooth(source, sides, matrix, go, pair):
        blocks = []
        for m in pair:
            blocks.append(jnp.concatenate([
                source[m, pl.ds(HALF * go, 3 * HALF)].reshape(3 * cells, levels),
                sides[0, m, pl.ds(go, 3)].reshape(3 * HALF * HALF, levels),
                sides[1, m, pl.ds(go, 3)].reshape(3 * HALF * HALF, levels),
            ], axis=0))
        both = dot(matrix[...], jnp.concatenate(blocks, axis=1))
        return both[:cells] + both[cells:]

    pairs = [tuple(range(m, m + width)) for m in range(0, members, width)]

    def forward(go, carry):
        total = None
        for pair in pairs:
            level = dot(smooth(ext, halo, filt, go, pair).astype(BF16), vert2[...])
            for j, m in enumerate(pair):
                spread = ens[m, pl.ds(HALF * go, HALF)].reshape(cells, levels).astype(F32)
                term = spread * level[:, j * levels : (j + 1) * levels]
                total = term if total is None else total + term
        own[go] = total
        inc_out[go] = total.astype(BF16)
        return carry

    received(side_flat, row_up + side_up, row_down + side_down)

    peers = n["mem"] - 1
    per = groups // chunks
    inc_copies = []
    for chunk in range(chunks):
        at = pl.ds(chunk * per, per)
        lax.fori_loop(chunk * per, (chunk + 1) * per, forward, 0, unroll=2)
        copies = []
        for step in range(1, n["mem"]):
            to = device(mem=lax.rem(me["mem"] + step, n["mem"]))
            copies.append(remote(
                inc_out.at[at], inc_in.at[step - 1, at],
                inc_send.at[step - 1, chunk], inc_recv.at[step - 1, chunk], to,
            ))
            copies[-1].start()
        inc_copies.append(copies)

    def squares(go, carry):
        total = sums[...]
        for m in range(members):
            block = ext[m, pl.ds(HALF * (go + 1), HALF)].reshape(cells, levels).astype(F32)
            total = total + tile_sum(block * block)
        sums[...] = total
        return carry

    lax.fori_loop(0, groups, squares, 0)

    def adjoint(go, carry):
        increment = own[go]
        for peer in range(peers):
            increment = increment + inc_in[peer, go].astype(F32)
        weighted = prec[pl.ds(HALF * go, HALF)].reshape(cells, levels) * increment
        sums[...] += tile_sum(weighted * increment) * (1.0 / n["mem"])
        blocks = []
        for pair in pairs:
            parts = []
            for m in pair:
                spread = ens[m, pl.ds(HALF * go, HALF)].reshape(cells, levels).astype(F32)
                parts.append((spread * weighted).astype(BF16))
            result = dot(jnp.concatenate(parts, axis=1), vert2t[...]).astype(BF16)
            for j, m in enumerate(pair):
                block = result[:, j * levels : (j + 1) * levels]
                ext2[m, pl.ds(HALF * (go + 1), HALF)] = block.reshape(HALF, cols, levels)
                blocks.append(block)
        pack(blocks, go, stage2)
        return carry

    for chunk in range(chunks):
        for copy in inc_copies[chunk]:
            copy.wait_recv()
        lax.fori_loop(chunk * per, (chunk + 1) * per, adjoint, 0, unroll=2)

    row2_up, row2_down = row_copies(
        1, ext2.at[:, pl.ds(HALF, HALF)], ext2.at[:, pl.ds(rows, HALF)], ext2
    )
    side2_flat, side2_up, side2_down = side_copies(1, stage2, halo2)
    start(side2_flat, row2_up + side2_up, row2_down + side2_down)

    def final(go, carry):
        for pair in pairs:
            back = smooth(ext2, halo2, filt2, go, pair)
            for j, m in enumerate(pair):
                held = ext[m, pl.ds(HALF * (go + 1), HALF)].astype(F32)
                block = back[:, j * levels : (j + 1) * levels].reshape(HALF, cols, levels)
                hess[m, pl.ds(HALF * go, HALF)] = held + block
        return carry

    partial = sums[...]
    for index, (axis, buf) in enumerate(zip(axes, (cs0, cs1, cs2))):
        mine = me[axis]
        buf[mine] = partial
        copies = []
        for step in range(1, n[axis]):
            to = lax.rem(mine + step, n[axis])
            copies.append(remote(
                buf.at[mine], buf.at[mine], cs_send.at[index, step - 1],
                cs_recv.at[index, mine], device(**{axis: to}),
            ))
            copies[-1].start()
        for step in range(1, n[axis]):
            source = lax.rem(mine + step, n[axis])
            remote(
                buf.at[source], buf.at[source], cs_send.at[index, step - 1],
                cs_recv.at[index, source], device(**{axis: source}),
            ).wait_recv()
        for copy in copies:
            copy.wait_send()
        partial = buf[0]
        for other in range(1, n[axis]):
            partial = partial + buf[other]
    curv[0, 0] = jnp.sum(partial) * (1.0 / entries)

    received(side2_flat, row2_up + side2_up, row2_down + side2_down)
    lax.fori_loop(0, groups, final, 0, unroll=2)

    sent(side_flat, row_up + side_up, row_down + side_down)
    sent(side2_flat, row2_up + side2_up, row2_down + side2_down)
    for copies in inc_copies:
        for copy in copies:
            copy.wait_send()


def per_device(axes, sizes, control, ensemble, precision, lat_taps, lon_taps, vertical):
    members, rows, cols, levels = control.shape
    n = dict(zip(axes, sizes))
    groups = rows // HALF
    cells = HALF * cols
    pack = HALF * HALF
    entries = control.size
    for size in sizes:
        entries *= size
    chunks = 4 if groups % 4 == 0 else 1
    width = 2 if members % 2 == 0 else 1
    inner = 3 * cells + 6 * pack
    smem = pl.BlockSpec(memory_space=pltpu.SMEM)
    anyspace = pl.BlockSpec(memory_space=pl.ANY)
    most = max(sizes)
    peers = max(n["mem"] - 1, 1)
    hessian, curvature = pl.pallas_call(
        functools.partial(kernel, axes, sizes, entries, chunks),
        out_shape=(
            jax.ShapeDtypeStruct(control.shape, F32),
            jax.ShapeDtypeStruct((1, 1), F32),
        ),
        in_specs=[smem, smem, anyspace, anyspace, anyspace, anyspace],
        out_specs=(pl.BlockSpec(memory_space=pltpu.VMEM), smem),
        scratch_shapes=[
            pltpu.VMEM((members, rows + 2 * HALF, cols, levels), BF16),
            pltpu.VMEM((members, rows + 2 * HALF, cols, levels), BF16),
            pltpu.VMEM(control.shape, BF16),
            pltpu.VMEM(precision.shape, F32),
            pltpu.VMEM((groups, cells, levels), F32),
            pltpu.VMEM((groups, cells, levels), BF16),
            pltpu.VMEM((peers, groups, cells, levels), BF16),
            pltpu.VMEM((2, members, groups + 2, pack, levels), BF16),
            pltpu.VMEM((2, members, groups + 2, pack, levels), BF16),
            pltpu.VMEM((2, members, groups, pack, levels), BF16),
            pltpu.VMEM((2, members, groups, pack, levels), BF16),
            pltpu.VMEM((2 * cells, inner), BF16),
            pltpu.VMEM((2 * cells, inner), BF16),
            pltpu.VMEM((2 * pack, cells), BF16),
            pltpu.VMEM((levels, levels), BF16),
            pltpu.VMEM((width * levels, width * levels), BF16),
            pltpu.VMEM((width * levels, width * levels), BF16),
            pltpu.VMEM((8, levels), F32),
            pltpu.VMEM((sizes[0], 8, levels), F32),
            pltpu.VMEM((sizes[1], 8, levels), F32),
            pltpu.VMEM((sizes[2], 8, levels), F32),
            pltpu.SemaphoreType.DMA((4,)),
            pltpu.SemaphoreType.DMA((2, 8)),
            pltpu.SemaphoreType.DMA((2, 8)),
            pltpu.SemaphoreType.DMA((peers, chunks)),
            pltpu.SemaphoreType.DMA((peers, chunks)),
            pltpu.SemaphoreType.DMA((len(axes), most)),
            pltpu.SemaphoreType.DMA((len(axes), most)),
        ],
        compiler_params=pltpu.CompilerParams(
            collective_id=0, has_side_effects=True, vmem_limit_bytes=60 * 1024 * 1024
        ),
    )(lat_taps, lon_taps, control, ensemble, precision, vertical)
    return hessian, curvature.reshape(())


def solution(mesh):
    axes = tuple(mesh.axis_names)
    sizes = tuple(mesh.shape[a] for a in axes)
    in_specs = (
        P("mem", "lat", "lon", None),
        P("mem", "lat", "lon", None),
        P("lat", "lon", None),
        P(),
        P(),
        P(),
    )
    out_specs = (P("mem", "lat", "lon", None), P())
    return jax.shard_map(
        functools.partial(per_device, axes, sizes),
        mesh=mesh, in_specs=in_specs, out_specs=out_specs, check_vma=False,
    )
```

time: 219 us -> 54.5 us (0.25)
  waiting for transfers between devices: 63.3 us -> 0 us
  other arithmetic: 57.2 us -> 0 us
  Pallas kernels: 0 us -> 47.3 us
  blocking collectives: 39.3 us -> 0 us
  matrix products: 24.8 us -> 0 us
  between operations: 16 us -> 2.38 us
  starting transfers between devices: 12.7 us -> 0 us
    pallas_call x0 -> x1, Pallas kernels: none -> 47.3 us  [per_device(): pl.pallas_call(functools.partial(kernel, axes, sizes, entries, chunks), o...]
    psum x1 -> x0, waiting for transfers between devices: 41.8 us -> none  [per_device(): increment = lax.psum(partial_value, 'mem')]
    psum x1 -> x0, blocking collectives: 39.3 us -> none  [per_device(): lax.psum(jnp.sum(control * hessian), ('mem', 'lat', 'lon')) / entries]
    reduce_sum x1 -> x0, other arithmetic: 27.1 us -> none  [per_device(): jnp.sum(control * hessian)]
    dot_general x2 -> x0, matrix products: 24.8 us -> none  [the longest x1 24 us: per_device(): jnp.dot(smoothed.reshape(-1, levels), vertical, preferred_element_type=jn...]
    add x2 -> x0, other arithmetic: 22.7 us -> none  [smooth_block(): across + first_taps[offset] * extended[:, offset:offset + tile_rows]]
    ppermute x8 -> x0, waiting for transfers between devices: 21.5 us -> none  [the longest x4 18.6 us: extended_2(): before = lax.ppermute(last, axis, up)]
    ppermute x8 -> x0, starting transfers between devices: 12.7 us -> none  [the longest x4 7.89 us: extended_2(): after = lax.ppermute(initial, axis, down)]
  transfers between devices with their start and end apart: 9 -> 0, of which waited for: 8 -> 0; matrix products, arithmetic and copies ran while one was open for 2% -> 0% of each run, Pallas kernels for 0% -> 0%
where the time goes in v1:
time: 54.5 us; the launch traced here: 54.3 us
  Pallas kernels  47.3 us (87%)
  local copies, waits for them, and re-layouts  4.64 us (9%)
  between operations  2.38 us (4%)
    pallas_call x1, Pallas kernels, per_device(): pl.pallas_call(functools.partial(kernel, axes, sizes, entries, chunks), o...  47.3 us
    unnamed x1, local copies, waits for them, and re-layouts  4.64 us

profile of v1, /device:TPU:0, one launch (start us, length us, event | category | flops | bytes accessed | tf_op | source)
XLA Modules:
  0.0 54.3 jit_solution(13932749655742400717)
XLA Ops:
  0.6 47.3 %shard_map.77 = (f32[4,64,32,128]{3,2,1,0:T(8,128)}, f32[1,1]{1,0:T(1,128)}) custom-call(f32[9]{0:T(128)} %lat_taps.1, f32[9]{0:T(128)} %lon_taps.1, bf16[4,64,32,128]{3,2,1,0:T(8,128)(2,1)} %control.1, bf16[4,64,32,128]{3,2,1,0:T(8,128)(2,1)} %ensemble.1, f32[64,32,128]{2,1,0:T(8,128)} %precision.1, bf16[128,128]{1,0:T(8,128)(2,1)} %vertical.1), custom_call_target="tpu_custom_call" | custom-call | tf_op jit(solution)/shard_map/pallas_call | solution.py:392
  47.9 4.6 %copy.10 = f32[4,64,32,128]{3,2,1,0:T(8,128)} copy(f32[4,64,32,128]{3,2,1,0:T(8,128)} %get-tuple-element.8) | data formatting | bytes 8388608

commit v2 on v1

--- a/solution.py
+++ b/solution.py
@@ -60,11 +60,12 @@
 def kernel(
     axes, sizes, entries, chunks, lat_taps, lon_taps, control, ensemble, precision, vertical, hess, curv,
     ext, ext2, ens, prec, own, inc_out, inc_in, halo, halo2, stage, stage2,
-    filt, filt2, picks, vert, vert2, vert2t, sums, cs0, cs1, cs2,
-    local_sem, send_sem, recv_sem, inc_send, inc_recv, cs_send, cs_recv,
+    outs, filt, filt2, picks, vert, vert2, vert2t, sums, cs0, cs1, cs2,
+    local_sem, send_sem, recv_sem, side_send, side_recv, inc_send, inc_recv, cs_send, cs_recv, out_sem,
 ):
     members, rows, cols, levels = control.shape
     groups = rows // HALF
+    per = groups // chunks
     cells = HALF * cols
     width = 2 if members % 2 == 0 else 1
     me = {a: lax.axis_index(a) for a in axes}
@@ -122,71 +123,56 @@
         )
         return [up], [down]
 
-    def side_copies(phase, src, dst):
-        flat, up, down = [], [], []
+    def corner_copies(phase, src, dst):
+        up, down = [], []
         for side, to in ((0, left), (1, right)):
             there = dst.at[1 - side]
             mine = src.at[side]
-            flat.append(remote(
-                mine, there.at[:, pl.ds(1, groups)],
-                send_sem.at[phase, 2 + side], recv_sem.at[phase, 2 + side], device(lon=to),
-            ))
             up.append(remote(
                 mine.at[:, 0], there.at[:, groups + 1],
-                send_sem.at[phase, 4 + side], recv_sem.at[phase, 4 + side], device(lat=lat - 1, lon=to),
+                send_sem.at[phase, 2 + side], recv_sem.at[phase, 2 + side], device(lat=lat - 1, lon=to),
             ))
             down.append(remote(
                 mine.at[:, groups - 1], there.at[:, 0],
-                send_sem.at[phase, 6 + side], recv_sem.at[phase, 6 + side], device(lat=lat + 1, lon=to),
+                send_sem.at[phase, 4 + side], recv_sem.at[phase, 4 + side], device(lat=lat + 1, lon=to),
             ))
-        return flat, up, down
-
-    def start(flat, up, down):
-        @pl.when(has_up)
+        return up, down
+
+    def side_copies(phase, src, dst, chunk):
+        return [
+            remote(
+                src.at[side, :, pl.ds(chunk * per, per)], dst.at[1 - side, :, pl.ds(chunk * per + 1, per)],
+                side_send.at[phase, side, chunk], side_recv.at[phase, side, chunk], device(lon=to),
+            )
+            for side, to in ((0, left), (1, right))
+        ]
+
+    def inc_copies(chunk):
+        at = pl.ds(chunk * per, per)
+        return [
+            remote(
+                inc_out.at[at], inc_in.at[step - 1, at],
+                inc_send.at[step - 1, chunk], inc_recv.at[step - 1, chunk],
+                device(mem=lax.rem(me["mem"] + step, n["mem"])),
+            )
+            for step in range(1, n["mem"])
+        ]
+
+    def out_copy(chunk):
+        at = pl.ds(chunk * per * HALF, per * HALF)
+        return pltpu.make_async_copy(outs.at[:, at], hess.at[:, at], out_sem.at[chunk])
+
+    def each(has, copies, act):
+        @pl.when(has)
         def _():
-            for copy in up:
-                copy.start()
-
-        @pl.when(has_down)
-        def _():
-            for copy in down:
-                copy.start()
-
-        for copy in flat:
-            copy.start()
-
-    def received(flat, up, down):
-        @pl.when(has_up)
-        def _():
-            for copy in down:
-                copy.wait_recv()
-
-        @pl.when(has_down)
-        def _():
-            for copy in up:
-                copy.wait_recv()
-
-        for copy in flat:
-            copy.wait_recv()
-
-    def sent(flat, up, down):
-        @pl.when(has_up)
-        def _():
-            for copy in up:
-                copy.wait_send()
-
-        @pl.when(has_down)
-        def _():
-            for copy in down:
-                copy.wait_send()
-
-        for copy in flat:
-            copy.wait_send()
+            for copy in copies:
+                getattr(copy, act)()
 
     row_up, row_down = row_copies(
         0, control.at[:, pl.ds(0, HALF)], control.at[:, pl.ds(rows - HALF, HALF)], ext
     )
-    start([], row_up, row_down)
+    each(has_up, row_up, "start")
+    each(has_down, row_down, "start")
 
     @pl.when(jnp.logical_not(has_up))
     def _():
@@ -219,8 +205,12 @@
         return carry
 
     lax.fori_loop(0, groups, pack_group, 0, unroll=2)
-    side_flat, side_up, side_down = side_copies(0, stage, halo)
-    start(side_flat, side_up, side_down)
+    corner_up, corner_down = corner_copies(0, stage, halo)
+    each(has_up, corner_up, "start")
+    each(has_down, corner_down, "start")
+    for chunk in range(chunks):
+        for copy in side_copies(0, stage, halo, chunk):
+            copy.start()
 
     filt[...] = filter_matrix(lat_taps, lon_taps, cols, False)
     filt2[...] = filter_matrix(lat_taps, lon_taps, cols, True)
@@ -239,11 +229,21 @@
     vert2[...] = diagonal(v)
     vert2t[...] = diagonal(vt)
     sums[...] = jnp.zeros_like(sums)
+
+    def tile_sum(x):
+        return jnp.sum(x.reshape(-1, 8, levels), axis=0)
+
+    def squares(go, carry):
+        total = sums[...]
+        for m in range(members):
+            block = ext[m, pl.ds(HALF * (go + 1), HALF)].reshape(cells, levels).astype(F32)
+            total = total + tile_sum(block * block)
+        sums[...] = total
+        return carry
+
+    lax.fori_loop(0, groups, squares, 0)
     loads[2].wait()
     loads[3].wait()
-
-    def tile_sum(x):
-        return jnp.sum(x.reshape(-1, 8, levels), axis=0)
 
     def smooth(source, sides, matrix, go, pair):
         blocks = []
@@ -258,7 +258,7 @@
 
     pairs = [tuple(range(m, m + width)) for m in range(0, members, width)]
 
-    def forward(go, carry):
+    def forward(go):
         total = None
         for pair in pairs:
             level = dot(smooth(ext, halo, filt, go, pair).astype(BF16), vert2[...])
@@ -268,37 +268,10 @@
                 total = term if total is None else total + term
         own[go] = total
         inc_out[go] = total.astype(BF16)
-        return carry
-
-    received(side_flat, row_up + side_up, row_down + side_down)
 
     peers = n["mem"] - 1
-    per = groups // chunks
-    inc_copies = []
-    for chunk in range(chunks):
-        at = pl.ds(chunk * per, per)
-        lax.fori_loop(chunk * per, (chunk + 1) * per, forward, 0, unroll=2)
-        copies = []
-        for step in range(1, n["mem"]):
-            to = device(mem=lax.rem(me["mem"] + step, n["mem"]))
-            copies.append(remote(
-                inc_out.at[at], inc_in.at[step - 1, at],
-                inc_send.at[step - 1, chunk], inc_recv.at[step - 1, chunk], to,
-            ))
-            copies[-1].start()
-        inc_copies.append(copies)
-
-    def squares(go, carry):
-        total = sums[...]
-        for m in range(members):
-            block = ext[m, pl.ds(HALF * (go + 1), HALF)].reshape(cells, levels).astype(F32)
-            total = total + tile_sum(block * block)
-        sums[...] = total
-        return carry
-
-    lax.fori_loop(0, groups, squares, 0)
-
-    def adjoint(go, carry):
+
+    def adjoint(go):
         increment = own[go]
         for peer in range(peers):
             increment = increment + inc_in[peer, go].astype(F32)
@@ -316,61 +289,129 @@
                 ext2[m, pl.ds(HALF * (go + 1), HALF)] = block.reshape(HALF, cols, levels)
                 blocks.append(block)
         pack(blocks, go, stage2)
-        return carry
-
-    for chunk in range(chunks):
-        for copy in inc_copies[chunk]:
-            copy.wait_recv()
-        lax.fori_loop(chunk * per, (chunk + 1) * per, adjoint, 0, unroll=2)
-
-    row2_up, row2_down = row_copies(
-        1, ext2.at[:, pl.ds(HALF, HALF)], ext2.at[:, pl.ds(rows, HALF)], ext2
-    )
-    side2_flat, side2_up, side2_down = side_copies(1, stage2, halo2)
-    start(side2_flat, row2_up + side2_up, row2_down + side2_down)
-
-    def final(go, carry):
+
+    def final(go):
         for pair in pairs:
             back = smooth(ext2, halo2, filt2, go, pair)
             for j, m in enumerate(pair):
                 held = ext[m, pl.ds(HALF * (go + 1), HALF)].astype(F32)
                 block = back[:, j * levels : (j + 1) * levels].reshape(HALF, cols, levels)
-                hess[m, pl.ds(HALF * go, HALF)] = held + block
-        return carry
-
-    partial = sums[...]
-    for index, (axis, buf) in enumerate(zip(axes, (cs0, cs1, cs2))):
+                outs[m, pl.ds(HALF * go, HALF)] = held + block
+
+    def of_chunk(work, chunk):
+        for g in range(per):
+            work(chunk * per + g)
+
+    def wait_sides(phase, src, dst, chunk):
+        for copy in side_copies(phase, src, dst, chunk):
+            copy.wait_recv()
+
+    def forward_chunk(chunk, carry):
+        of_chunk(forward, chunk)
+        for copy in inc_copies(chunk):
+            copy.start()
+        return carry
+
+    def forward_wait(chunk, carry):
+        wait_sides(0, stage, halo, chunk + 1)
+        return forward_chunk(chunk, carry)
+
+    each(has_up, row_down + corner_down, "wait_recv")
+    each(has_down, row_up + corner_up, "wait_recv")
+    wait_sides(0, stage, halo, 0)
+    lax.fori_loop(0, chunks - 1, forward_wait, 0)
+    forward_chunk(chunks - 1, 0)
+
+    row2_up, row2_down = row_copies(
+        1, ext2.at[:, pl.ds(HALF, HALF)], ext2.at[:, pl.ds(rows, HALF)], ext2
+    )
+    corner2_up, corner2_down = corner_copies(1, stage2, halo2)
+
+    def adjoint_chunk(chunk, carry):
+        for copy in inc_copies(chunk):
+            copy.wait_recv()
+        of_chunk(adjoint, chunk)
+        each(jnp.logical_and(has_up, chunk == 0), row2_up + corner2_up, "start")
+        each(jnp.logical_and(has_down, chunk == chunks - 1), row2_down + corner2_down, "start")
+        for copy in side_copies(1, stage2, halo2, chunk):
+            copy.start()
+        return carry
+
+    def final_chunk(chunk, carry):
+        of_chunk(final, chunk)
+        out_copy(chunk).start()
+        return carry
+
+    def final_wait(chunk, carry):
+        wait_sides(1, stage2, halo2, chunk + 1)
+        return final_chunk(chunk, carry)
+
+    lag = min(4, chunks - 2)
+
+    def both_chunks(chunk, carry):
+        adjoint_chunk(chunk, carry)
+        return final_wait(chunk - lag, carry)
+
+    lax.fori_loop(0, lag + 1, adjoint_chunk, 0)
+    wait_sides(1, stage2, halo2, 0)
+    wait_sides(1, stage2, halo2, 1)
+    lax.fori_loop(lag + 1, chunks, both_chunks, 0)
+
+    bufs = (cs0, cs1, cs2)
+
+    def reduce_copies(index):
+        axis, buf = axes[index], bufs[index]
         mine = me[axis]
-        buf[mine] = partial
-        copies = []
+        out, arrive = [], []
         for step in range(1, n[axis]):
-            to = lax.rem(mine + step, n[axis])
-            copies.append(remote(
-                buf.at[mine], buf.at[mine], cs_send.at[index, step - 1],
-                cs_recv.at[index, mine], device(**{axis: to}),
-            ))
-            copies[-1].start()
-        for step in range(1, n[axis]):
-            source = lax.rem(mine + step, n[axis])
-            remote(
-                buf.at[source], buf.at[source], cs_send.at[index, step - 1],
-                cs_recv.at[index, source], device(**{axis: source}),
-            ).wait_recv()
-        for copy in copies:
+            other = lax.rem(mine + step, n[axis])
+            to = device(**{axis: other})
+            sem = cs_send.at[index, step - 1]
+            out.append(remote(buf.at[mine], buf.at[mine], sem, cs_recv.at[index, mine], to))
+            arrive.append(remote(buf.at[other], buf.at[other], sem, cs_recv.at[index, other], to))
+        return out, arrive
+
+    def reduce_start(index, partial):
+        bufs[index][me[axes[index]]] = partial
+        for copy in reduce_copies(index)[0]:
+            copy.start()
+
+    def reduce_end(index):
+        out, arrive = reduce_copies(index)
+        for copy in arrive:
+            copy.wait_recv()
+        for copy in out:
             copy.wait_send()
-        partial = buf[0]
-        for other in range(1, n[axis]):
-            partial = partial + buf[other]
-    curv[0, 0] = jnp.sum(partial) * (1.0 / entries)
-
-    received(side2_flat, row2_up + side2_up, row2_down + side2_down)
-    lax.fori_loop(0, groups, final, 0, unroll=2)
-
-    sent(side_flat, row_up + side_up, row_down + side_down)
-    sent(side2_flat, row2_up + side2_up, row2_down + side2_down)
-    for copies in inc_copies:
-        for copy in copies:
+        partial = bufs[index][0]
+        for other in range(1, n[axes[index]]):
+            partial = partial + bufs[index][other]
+        return partial
+
+    reduce_start(0, sums[...])
+    rest = chunks - lag
+    middle = rest + (lag - 1) // 2
+    lax.fori_loop(rest, middle, final_wait, 0)
+    reduce_start(1, reduce_end(0))
+    lax.fori_loop(middle, chunks - 1, final_wait, 0)
+    each(has_down, row2_up + corner2_up, "wait_recv")
+    final_chunk(chunks - 1, 0)
+    reduce_start(2, reduce_end(1))
+    each(has_up, row2_down + corner2_down, "wait_recv")
+    final_chunk(0, 0)
+    curv[0, 0] = jnp.sum(reduce_end(2)) * (1.0 / entries)
+
+    each(has_up, row_up + corner_up + row2_up + corner2_up, "wait_send")
+    each(has_down, row_down + corner_down + row2_down + corner2_down, "wait_send")
+
+    def finish(chunk, carry):
+        for copy in side_copies(0, stage, halo, chunk) + side_copies(1, stage2, halo2, chunk):
             copy.wait_send()
+        for copy in inc_copies(chunk):
+            copy.wait_send()
+        out_copy(chunk).wait()
+        return carry
+
+    lax.fori_loop(0, chunks, finish, 0)
 
 
 def per_device(axes, sizes, control, ensemble, precision, lat_taps, lon_taps, vertical):
@@ -382,7 +423,7 @@
     entries = control.size
     for size in sizes:
         entries *= size
-    chunks = 4 if groups % 4 == 0 else 1
+    chunks = next(c for c in (8, 4, groups) if groups % c == 0)
     width = 2 if members % 2 == 0 else 1
     inner = 3 * cells + 6 * pack
     smem = pl.BlockSpec(memory_space=pltpu.SMEM)
@@ -396,7 +437,7 @@
             jax.ShapeDtypeStruct((1, 1), F32),
         ),
         in_specs=[smem, smem, anyspace, anyspace, anyspace, anyspace],
-        out_specs=(pl.BlockSpec(memory_space=pltpu.VMEM), smem),
+        out_specs=(anyspace, smem),
         scratch_shapes=[
             pltpu.VMEM((members, rows + 2 * HALF, cols, levels), BF16),
             pltpu.VMEM((members, rows + 2 * HALF, cols, levels), BF16),
@@ -409,6 +450,7 @@
             pltpu.VMEM((2, members, groups + 2, pack, levels), BF16),
             pltpu.VMEM((2, members, groups, pack, levels), BF16),
             pltpu.VMEM((2, members, groups, pack, levels), BF16),
+            pltpu.VMEM(control.shape, F32),
             pltpu.VMEM((2 * cells, inner), BF16),
             pltpu.VMEM((2 * cells, inner), BF16),
             pltpu.VMEM((2 * pack, cells), BF16),
@@ -420,12 +462,15 @@
             pltpu.VMEM((sizes[1], 8, levels), F32),
             pltpu.VMEM((sizes[2], 8, levels), F32),
             pltpu.SemaphoreType.DMA((4,)),
-            pltpu.SemaphoreType.DMA((2, 8)),
-            pltpu.SemaphoreType.DMA((2, 8)),
+            pltpu.SemaphoreType.DMA((2, 6)),
+            pltpu.SemaphoreType.DMA((2, 6)),
+            pltpu.SemaphoreType.DMA((2, 2, chunks)),
+            pltpu.SemaphoreType.DMA((2, 2, chunks)),
             pltpu.SemaphoreType.DMA((peers, chunks)),
             pltpu.SemaphoreType.DMA((peers, chunks)),
             pltpu.SemaphoreType.DMA((len(axes), most)),
             pltpu.SemaphoreType.DMA((len(axes), most)),
+            pltpu.SemaphoreType.DMA((chunks,)),
         ],
         compiler_params=pltpu.CompilerParams(
             collective_id=0, has_side_effects=True, vmem_limit_bytes=60 * 1024 * 1024

time: 54.5 us -> 46.2 us (0.85)
  Pallas kernels: 47.3 us -> 39 us
    pallas_call x1, Pallas kernels: 47.3 us -> 39 us  [per_device(): pl.pallas_call(functools.partial(kernel, axes, sizes, entries, chunks), o...]
where the time goes in v2:
time: 46.2 us; the launch traced here: 46 us
  Pallas kernels  39 us (84%)
  local copies, waits for them, and re-layouts  4.64 us (10%)
  between operations  2.38 us (5%)
    pallas_call x1, Pallas kernels, per_device(): pl.pallas_call(functools.partial(kernel, axes, sizes, entries, chunks), o...  39 us
    unnamed x1, local copies, waits for them, and re-layouts  4.64 us

profile of v2, /device:TPU:0, one launch (start us, length us, event | category | flops | bytes accessed | tf_op | source)
XLA Modules:
  0.0 46.0 jit_solution(12587226965147184077)
XLA Ops:
  0.6 39.0 %shard_map.77 = (f32[4,64,32,128]{3,2,1,0:T(8,128)}, f32[1,1]{1,0:T(1,128)}) custom-call(f32[9]{0:T(128)} %lat_taps.1, f32[9]{0:T(128)} %lon_taps.1, bf16[4,64,32,128]{3,2,1,0:T(8,128)(2,1)} %control.1, bf16[4,64,32,128]{3,2,1,0:T(8,128)(2,1)} %ensemble.1, f32[64,32,128]{2,1,0:T(8,128)} %precision.1, bf16[128,128]{1,0:T(8,128)(2,1)} %vertical.1), custom_call_target="tpu_custom_call" | custom-call | tf_op jit(solution)/shard_map/pallas_call | solution.py:433
  39.6 4.6 %copy.10 = f32[4,64,32,128]{3,2,1,0:T(8,128)} copy(f32[4,64,32,128]{3,2,1,0:T(8,128)} %get-tuple-element.8) | data formatting | bytes 8388608

commit v3 on v2

--- a/solution.py
+++ b/solution.py
@@ -60,8 +60,8 @@
 def kernel(
     axes, sizes, entries, chunks, lat_taps, lon_taps, control, ensemble, precision, vertical, hess, curv,
     ext, ext2, ens, prec, own, inc_out, inc_in, halo, halo2, stage, stage2,
-    outs, filt, filt2, picks, vert, vert2, vert2t, sums, cs0, cs1, cs2,
-    local_sem, send_sem, recv_sem, side_send, side_recv, inc_send, inc_recv, cs_send, cs_recv, out_sem,
+    filt, filt2, picks, vert, vert2, vert2t, sums, cs0, cs1, cs2,
+    local_sem, send_sem, recv_sem, side_send, side_recv, inc_send, inc_recv, cs_send, cs_recv,
 ):
     members, rows, cols, levels = control.shape
     groups = rows // HALF
@@ -158,10 +158,6 @@
             for step in range(1, n["mem"])
         ]
 
-    def out_copy(chunk):
-        at = pl.ds(chunk * per * HALF, per * HALF)
-        return pltpu.make_async_copy(outs.at[:, at], hess.at[:, at], out_sem.at[chunk])
-
     def each(has, copies, act):
         @pl.when(has)
         def _():
@@ -271,12 +267,16 @@
 
     peers = n["mem"] - 1
 
-    def adjoint(go):
+    def weigh(go):
         increment = own[go]
         for peer in range(peers):
             increment = increment + inc_in[peer, go].astype(F32)
         weighted = prec[pl.ds(HALF * go, HALF)].reshape(cells, levels) * increment
         sums[...] += tile_sum(weighted * increment) * (1.0 / n["mem"])
+        own[go] = weighted
+
+    def adjoint(go):
+        weighted = own[go]
         blocks = []
         for pair in pairs:
             parts = []
@@ -296,7 +296,7 @@
             for j, m in enumerate(pair):
                 held = ext[m, pl.ds(HALF * (go + 1), HALF)].astype(F32)
                 block = back[:, j * levels : (j + 1) * levels].reshape(HALF, cols, levels)
-                outs[m, pl.ds(HALF * go, HALF)] = held + block
+                hess[m, pl.ds(HALF * go, HALF)] = held + block
 
     def of_chunk(work, chunk):
         for g in range(per):
@@ -327,9 +327,17 @@
     )
     corner2_up, corner2_down = corner_copies(1, stage2, halo2)
 
-    def adjoint_chunk(chunk, carry):
+    def weigh_chunk(chunk, carry):
         for copy in inc_copies(chunk):
             copy.wait_recv()
+        of_chunk(weigh, chunk)
+        return carry
+
+    def weigh_adjoint(chunk, carry):
+        weigh_chunk(chunk, carry)
+        return adjoint_chunk(chunk, carry)
+
+    def adjoint_chunk(chunk, carry):
         of_chunk(adjoint, chunk)
         each(jnp.logical_and(has_up, chunk == 0), row2_up + corner2_up, "start")
         each(jnp.logical_and(has_down, chunk == chunks - 1), row2_down + corner2_down, "start")
@@ -339,7 +347,6 @@
 
     def final_chunk(chunk, carry):
         of_chunk(final, chunk)
-        out_copy(chunk).start()
         return carry
 
     def final_wait(chunk, carry):
@@ -351,11 +358,6 @@
     def both_chunks(chunk, carry):
         adjoint_chunk(chunk, carry)
         return final_wait(chunk - lag, carry)
-
-    lax.fori_loop(0, lag + 1, adjoint_chunk, 0)
-    wait_sides(1, stage2, halo2, 0)
-    wait_sides(1, stage2, halo2, 1)
-    lax.fori_loop(lag + 1, chunks, both_chunks, 0)
 
     bufs = (cs0, cs1, cs2)
 
@@ -387,15 +389,20 @@
             partial = partial + bufs[index][other]
         return partial
 
+    lax.fori_loop(0, lag + 1, weigh_adjoint, 0)
+    lax.fori_loop(lag + 1, chunks, weigh_chunk, 0)
     reduce_start(0, sums[...])
+    wait_sides(1, stage2, halo2, 0)
+    wait_sides(1, stage2, halo2, 1)
+    lax.fori_loop(lag + 1, chunks, both_chunks, 0)
+    reduce_start(1, reduce_end(0))
     rest = chunks - lag
-    middle = rest + (lag - 1) // 2
+    middle = rest + (lag - 1) // 2 + 1
     lax.fori_loop(rest, middle, final_wait, 0)
-    reduce_start(1, reduce_end(0))
+    reduce_start(2, reduce_end(1))
     lax.fori_loop(middle, chunks - 1, final_wait, 0)
     each(has_down, row2_up + corner2_up, "wait_recv")
     final_chunk(chunks - 1, 0)
-    reduce_start(2, reduce_end(1))
     each(has_up, row2_down + corner2_down, "wait_recv")
     final_chunk(0, 0)
     curv[0, 0] = jnp.sum(reduce_end(2)) * (1.0 / entries)
@@ -408,7 +415,6 @@
             copy.wait_send()
         for copy in inc_copies(chunk):
             copy.wait_send()
-        out_copy(chunk).wait()
         return carry
 
     lax.fori_loop(0, chunks, finish, 0)
@@ -427,17 +433,17 @@
     width = 2 if members % 2 == 0 else 1
     inner = 3 * cells + 6 * pack
     smem = pl.BlockSpec(memory_space=pltpu.SMEM)
-    anyspace = pl.BlockSpec(memory_space=pl.ANY)
+    anyspace = pl.BlockSpec(memory_space=pltpu.HBM)
     most = max(sizes)
     peers = max(n["mem"] - 1, 1)
     hessian, curvature = pl.pallas_call(
         functools.partial(kernel, axes, sizes, entries, chunks),
         out_shape=(
-            jax.ShapeDtypeStruct(control.shape, F32),
+            pltpu.VMEM(control.shape, F32),
             jax.ShapeDtypeStruct((1, 1), F32),
         ),
         in_specs=[smem, smem, anyspace, anyspace, anyspace, anyspace],
-        out_specs=(anyspace, smem),
+        out_specs=(pl.BlockSpec(memory_space=pltpu.VMEM), smem),
         scratch_shapes=[
             pltpu.VMEM((members, rows + 2 * HALF, cols, levels), BF16),
             pltpu.VMEM((members, rows + 2 * HALF, cols, levels), BF16),
@@ -450,7 +456,6 @@
             pltpu.VMEM((2, members, groups + 2, pack, levels), BF16),
             pltpu.VMEM((2, members, groups, pack, levels), BF16),
             pltpu.VMEM((2, members, groups, pack, levels), BF16),
-            pltpu.VMEM(control.shape, F32),
             pltpu.VMEM((2 * cells, inner), BF16),
             pltpu.VMEM((2 * cells, inner), BF16),
             pltpu.VMEM((2 * pack, cells), BF16),
@@ -470,10 +475,9 @@
             pltpu.SemaphoreType.DMA((peers, chunks)),
             pltpu.SemaphoreType.DMA((len(axes), most)),
             pltpu.SemaphoreType.DMA((len(axes), most)),
-            pltpu.SemaphoreType.DMA((chunks,)),
         ],
         compiler_params=pltpu.CompilerParams(
-            collective_id=0, has_side_effects=True, vmem_limit_bytes=60 * 1024 * 1024
+            collective_id=0, has_side_effects=True, vmem_limit_bytes=59 * 1024 * 1024
         ),
     )(lat_taps, lon_taps, control, ensemble, precision, vertical)
     return hessian, curvature.reshape(())

time: 46.2 us -> 42.3 us (0.916)
  local copies, waits for them, and re-layouts: 4.64 us -> 2.02 us
  Pallas kernels: 39 us -> 37.7 us
    unnamed x1, local copies, waits for them, and re-layouts: 4.64 us -> 2.02 us
    pallas_call x1, Pallas kernels: 39 us -> 37.7 us  [per_device(): pl.pallas_call(functools.partial(kernel, axes, sizes, entries, chunks), o...]
where the time goes in v3:
time: 42.3 us; the launch traced here: 42.1 us
  Pallas kernels  37.7 us (89%)
  between operations  2.33 us (6%)
  local copies, waits for them, and re-layouts  2.02 us (5%)
    pallas_call x1, Pallas kernels, per_device(): pl.pallas_call(functools.partial(kernel, axes, sizes, entries, chunks), o...  37.7 us
    unnamed x1, local copies, waits for them, and re-layouts  2.02 us

profile of v3, /device:TPU:0, one launch (start us, length us, event | category | flops | bytes accessed | tf_op | source)
XLA Modules:
  0.0 42.1 jit_solution(17267273441632505287)
XLA Ops:
  0.6 37.7 %shard_map.77 = (f32[4,64,32,128]{3,2,1,0:T(8,128)S(1)}, f32[1,1]{1,0:T(1,128)}) custom-call(f32[9]{0:T(128)} %lat_taps.1, f32[9]{0:T(128)} %lon_taps.1, bf16[4,64,32,128]{3,2,1,0:T(8,128)(2,1)} %control.1, bf16[4,64,32,128]{3,2,1,0:T(8,128)(2,1)} %ensemble.1, f32[64,32,128]{2,1,0:T(8,128)} %precision.1, bf16[128,128]{1,0:T(8,128)(2,1)} %vertical.1), custom_call_target="tpu_custom_call" | custom-call | tf_op jit(solution)/shard_map/pallas_call | solution.py:439
  38.4 2.0 %copy.10 = f32[4,64,32,128]{3,2,1,0:T(8,128)} copy(f32[4,64,32,128]{3,2,1,0:T(8,128)S(1)} %get-tuple-element.6) | data formatting | bytes 8388608

commit v4 on v3

--- a/solution.py
+++ b/solution.py
@@ -254,16 +254,19 @@
 
     pairs = [tuple(range(m, m + width)) for m in range(0, members, width)]
 
-    def forward(go):
-        total = None
-        for pair in pairs:
-            level = dot(smooth(ext, halo, filt, go, pair).astype(BF16), vert2[...])
-            for j, m in enumerate(pair):
-                spread = ens[m, pl.ds(HALF * go, HALF)].reshape(cells, levels).astype(F32)
-                term = spread * level[:, j * levels : (j + 1) * levels]
-                total = term if total is None else total + term
-        own[go] = total
-        inc_out[go] = total.astype(BF16)
+    def forward(chunk):
+        places = [chunk * per + g for g in range(per)]
+        smoothed = [[smooth(ext, halo, filt, go, pair).astype(BF16) for pair in pairs] for go in places]
+        for go, held in zip(places, smoothed):
+            total = None
+            for pair, value in zip(pairs, held):
+                level = dot(value, vert2[...])
+                for j, m in enumerate(pair):
+                    spread = ens[m, pl.ds(HALF * go, HALF)].reshape(cells, levels).astype(F32)
+                    term = spread * level[:, j * levels : (j + 1) * levels]
+                    total = term if total is None else total + term
+            own[go] = total
+            inc_out[go] = total.astype(BF16)
 
     peers = n["mem"] - 1
 
@@ -307,7 +310,7 @@
             copy.wait_recv()
 
     def forward_chunk(chunk, carry):
-        of_chunk(forward, chunk)
+        forward(chunk)
         for copy in inc_copies(chunk):
             copy.start()
         return carry

time: 42.3 us -> 41.6 us (0.983)
  Pallas kernels: 37.7 us -> 37 us
    pallas_call x1, Pallas kernels: 37.7 us -> 37 us  [per_device(): pl.pallas_call(functools.partial(kernel, axes, sizes, entries, chunks), o...]
where the time goes in v4:
time: 41.6 us; the launch traced here: 41.4 us
  Pallas kernels  37 us (89%)
  between operations  2.33 us (6%)
  local copies, waits for them, and re-layouts  2.02 us (5%)
    pallas_call x1, Pallas kernels, per_device(): pl.pallas_call(functools.partial(kernel, axes, sizes, entries, chunks), o...  37 us
    unnamed x1, local copies, waits for them, and re-layouts  2.02 us

profile of v4, /device:TPU:0, one launch (start us, length us, event | category | flops | bytes accessed | tf_op | source)
XLA Modules:
  0.0 41.4 jit_solution(410624995709235055)
XLA Ops:
  0.6 37.0 %shard_map.77 = (f32[4,64,32,128]{3,2,1,0:T(8,128)S(1)}, f32[1,1]{1,0:T(1,128)}) custom-call(f32[9]{0:T(128)} %lat_taps.1, f32[9]{0:T(128)} %lon_taps.1, bf16[4,64,32,128]{3,2,1,0:T(8,128)(2,1)} %control.1, bf16[4,64,32,128]{3,2,1,0:T(8,128)(2,1)} %ensemble.1, f32[64,32,128]{2,1,0:T(8,128)} %precision.1, bf16[128,128]{1,0:T(8,128)(2,1)} %vertical.1), custom_call_target="tpu_custom_call" | custom-call | tf_op jit(solution)/shard_map/pallas_call | solution.py:442
  37.7 2.0 %copy.10 = f32[4,64,32,128]{3,2,1,0:T(8,128)} copy(f32[4,64,32,128]{3,2,1,0:T(8,128)S(1)} %get-tuple-element.6) | data formatting | bytes 8388608
